TPU v7x, 128 devices: a whole 4x4x4 slice. The times are simulated.
128 devices in a mesh: front: 4 (over y), row: 8 (over z, x_lo), col: 4 (over x_hi, core).
Axes of the slice: x: 4 (x_hi: 2, x_lo: 2; x = x_hi * 2 + x_lo), y: 4, z: 4, core: 2. Of those that a mesh axis runs over, the one named last changes fastest.
Arguments:
- front_entries: bfloat16 [36864, 9216], P(('front', 'row'), 'col'), parts along dimension 0, as said below
- children: bfloat16 [8, 8192, 8192], P('front', 'row', 'col'), parts along dimension 0, as said below
- child_maps: int32 [8, 64], P('front'), parts along dimension 0, may hold values from 0 to 71, as said below
Outputs:
- factor: float32 [36864, 9216], P(('front', 'row'), 'col'), parts along dimension 0
There are 4 independent parts, one for each index of `front`. A program takes and returns all parts, laid end to end along the dimension named above; each array names one. Nothing has to cross between parts.
Inputs may be any that keep to these rules, and one draw needn't show every extreme that they name: `front_entries`: symmetric in natural order; the leading 256 x 256 block of the matrix assembled by the steps is positive definite. `children`: each child's matrix is symmetric in natural order. `child_maps`: the entries of one child are distinct. For each child, among its blocks k with k mod 8 = a, exactly 1 has a value v with v mod 8 = d, for every a and d; and among its blocks k with k mod 4 = a, exactly 4 have a value v with v mod 4 = d, for every a and d.
All inputs are finite; a program needn't handle non-finite values.
Results may differ from a plain program's by a relative error of at most 0.0003.
Values may be sent and summed in bfloat16 or wider, within the bound.
A program may use at most 128 MiB of HBM per device.

v0:
```python
import jax
import jax.numpy as jnp
from jax import lax
from jax.sharding import PartitionSpec as P

BLK = 128
SEP = 256


def broadcast(value, axis, source):
    kept = jnp.where(lax.axis_index(axis) == source, value, 0).astype(value.dtype)
    return lax.psum(kept, axis)


def arrivals(child_maps, axis_size, own_index, blocks):
    local_ids = jnp.arange(blocks, dtype=jnp.int32)
    source = jnp.arange(axis_size, dtype=jnp.int32)
    parents = child_maps[:, local_ids[None, :] * axis_size + source[:, None]]
    ranking = jnp.argsort(
        jnp.where(parents % axis_size == own_index, 0, 1) * blocks + local_ids, axis=2
    )
    chosen = jnp.take_along_axis(parents, ranking[:, :, : blocks // axis_size], axis=2)
    return (chosen // axis_size).reshape(parents.shape[0], -1)


def sending_order(child_maps, axis_size, own_index, blocks):
    local_ids = jnp.arange(blocks, dtype=jnp.int32)
    parents = child_maps[:, local_ids * axis_size + own_index]
    return jnp.argsort(parents % axis_size * blocks + local_ids[None, :], axis=1)


def shards(front_entries, children, child_maps):
    rows_axis = lax.axis_size("row")
    cols_axis = lax.axis_size("col")
    own_row = lax.axis_index("row")
    own_col = lax.axis_index("col")
    front_rows = front_entries.shape[0] // BLK
    front_cols = front_entries.shape[1] // BLK
    child_rows = children.shape[1] // BLK
    child_cols = children.shape[2] // BLK
    row_sends = child_rows // rows_axis
    col_sends = child_cols // cols_axis
    row_order = sending_order(child_maps, rows_axis, own_row, child_rows)
    col_order = sending_order(child_maps, cols_axis, own_col, child_cols)
    tile_grid = children.reshape(2, child_rows, BLK, child_cols, BLK)
    tile_grid = jnp.take_along_axis(tile_grid, row_order[:, :, None, None, None], axis=1)
    tile_grid = jnp.take_along_axis(tile_grid, col_order[:, None, None, :, None], axis=3)
    tile_grid = tile_grid.reshape(2, rows_axis, row_sends, BLK, cols_axis, col_sends, BLK)
    outgoing = tile_grid.transpose(0, 1, 4, 2, 3, 5, 6).reshape(
        2, rows_axis * cols_axis, row_sends, BLK, col_sends, BLK
    )
    incoming = lax.all_to_all(outgoing, ("row", "col"), split_axis=1, concat_axis=1, tiled=True)
    incoming = incoming.reshape(2, rows_axis, cols_axis, row_sends, BLK, col_sends, BLK)
    arrived = incoming.transpose(0, 1, 3, 4, 2, 5, 6)
    arrived = arrived.reshape(2, child_rows, BLK, child_cols, BLK)
    row_dest = arrivals(child_maps, rows_axis, own_row, child_rows)
    col_dest = arrivals(child_maps, cols_axis, own_col, child_cols)
    assembled = front_entries.astype(jnp.float32).reshape(front_rows, BLK, front_cols, BLK)
    for child_index in range(2):
        addend = arrived[child_index].transpose(0, 2, 1, 3).astype(jnp.float32)
        assembled = assembled.at[
            row_dest[child_index][:, None], :, col_dest[child_index][None, :], :
        ].add(addend)
    assembled = assembled.reshape(front_rows * BLK, front_cols * BLK)
    row_blocks = jnp.arange(front_rows, dtype=jnp.int32) * rows_axis + own_row
    col_blocks = jnp.arange(front_cols, dtype=jnp.int32) * cols_axis + own_col
    spread = rows_axis // cols_axis

    def eliminate(pivot_index, current_front):
        col_slot = pivot_index // cols_axis
        column = lax.dynamic_slice_in_dim(current_front, col_slot * BLK, BLK, 1)
        column = broadcast(column, "col", pivot_index % cols_axis)
        diag_block = lax.dynamic_slice_in_dim(column, pivot_index // rows_axis * BLK, BLK, 0)
        diag_block = broadcast(diag_block, "row", pivot_index % rows_axis)
        diag_factor = jnp.tril(jnp.linalg.cholesky(diag_block))
        solved = lax.linalg.triangular_solve(
            diag_factor, column, left_side=False, lower=True, transpose_a=True
        )
        panel_tiles = solved.reshape(front_rows, BLK, BLK)
        panel_tiles = jnp.where(
            (row_blocks == pivot_index)[:, None, None], diag_factor[None], panel_tiles
        )
        stored_col = jnp.where(
            (row_blocks >= pivot_index)[:, None, None], panel_tiles, 0.0
        ).reshape(front_rows * BLK, BLK)
        below_rows = jnp.where((row_blocks > pivot_index)[:, None, None], panel_tiles, 0.0).reshape(
            front_rows * BLK, BLK
        )
        received = [
            broadcast(below_rows, "row", own_col + offset * cols_axis).reshape(front_rows, BLK, BLK)
            for offset in range(spread)
        ]
        across_cols = jnp.stack(received, axis=1).reshape(front_cols * BLK, BLK)
        updated = current_front - lax.dot_general(
            below_rows,
            across_cols,
            (((1,), (1,)), ((), ())),
            precision=lax.Precision.HIGHEST,
            preferred_element_type=jnp.float32,
        )
        present = lax.dynamic_slice_in_dim(updated, col_slot * BLK, BLK, 1)
        column_new = jnp.where(own_col == pivot_index % cols_axis, stored_col, present)
        return lax.dynamic_update_slice_in_dim(updated, column_new, col_slot * BLK, 1)

    finished = lax.fori_loop(0, SEP // BLK, eliminate, assembled)
    upper_mask = (row_blocks < SEP // BLK)[:, None] & (col_blocks >= SEP // BLK)[None, :]
    finished = finished.reshape(front_rows, BLK, front_cols, BLK)
    finished = jnp.where(upper_mask[:, None, :, None], 0.0, finished)
    return finished.reshape(front_rows * BLK, front_cols * BLK)


def solution(mesh):
    in_specs = (P(("front", "row"), "col"), P("front", "row", "col"), P("front", None))
    out_specs = P(("front", "row"), "col")
    return jax.shard_map(shards, mesh=mesh, in_specs=in_specs, out_specs=out_specs, check_vma=False)
```

profile of v0, /device:TPU:0, one launch (start us, length us, event | category | flops | bytes accessed | tf_op | source)
XLA Modules:
  0.0 783.9 jit_solution(9959633989343557825)
XLA Ops:
  6.5 0.8 copy.77
  7.3 0.6 gather_fusion.3
  7.9 0.7 sort.71
  8.6 0.6 gather_fusion.2
  9.2 0.7 sort.70
  10.0 0.6 gather_fusion
  10.9 0.7 sort.68
  11.7 9.9 %copy.114 = bf16[256,8,16,128]{3,2,1,0:T(8,128)(2,1)} copy(bf16[256,8,16,128]{3,1,2,0:T(8,128)(2,1)} %bitcast.166) | data formatting | bytes 16777216
  22.0 8.3 %gather_fusion.6 = bf16[16,128,16,128]{3,2,1,0:T(8,128)(2,1)} fusion(bf16[2,8,128,16,128]{4,3,2,1,0:T(8,128)(2,1)} %bitcast.158, s32[16]{0:T(128)S(1)} %reshape.558), kind=kCustom, calls=%fused_computation.6 | custom fusion | bytes 16777344 | tf_op jit(solution)/shard_map/jit(take_along_axis)/gather | solution.py:46
  30.3 8.8 %copy_select_fusion = bf16[2,8,128,16,128]{4,2,3,1,0:T(8,128)(2,1)} fusion(bf16[2,8,128,16,128]{4,3,2,1,0:T(8,128)(2,1)} %bitcast.159, pred[2,8]{1,0:T(4,128)(4,1)S(1)} %copy.93), kind=kLoop, calls=%fused_computation.37 | loop fusion | flops 4194304 | bytes 16777232 | tf_op jit(solution)/shard_map/jit(take_along_axis)/select_n | solution.py:46
  39.1 8.6 %gather_fusion.7 = bf16[32,8,128,128]{3,2,1,0:T(8,128)(2,1)} fusion(bf16[2,8,128,16,128]{4,2,3,1,0:T(8,128)(2,1)} %copy_select_fusion, s32[32]{0:T(128)S(1)} %reshape.564), kind=kCustom, calls=%fused_computation.7 | custom fusion | bytes 16777472 | tf_op jit(solution)/shard_map/jit(take_along_axis)/gather | solution.py:47
  47.7 10.5 %copy.98 = bf16[2,8,128,16,128]{4,2,3,1,0:T(8,128)(2,1)} copy(bf16[2,8,128,16,128]{4,2,1,3,0:T(8,128)(2,1)} %bitcast.157) | data formatting | bytes 16777216 | tf_op jit(solution)/shard_map/jit(take_along_axis)/gather | solution.py:47
  58.3 7.7 broadcast_select_fusion.4
  66.0 10.5 %copy.99 = bf16[2,32,1,128,4,128]{5,3,4,2,0,1:T(8,128)(2,1)} copy(bf16[2,32,1,128,4,128]{5,3,4,2,1,0:T(8,128)(2,1)} %bitcast.161) | data formatting | bytes 16777216 | tf_op jit(solution)/shard_map/reshape | solution.py:49
  76.5 8.4 %all-to-all-start = ((bf16[2,32,1,128,4,128]{5,3,4,2,0,1:T(8,128)(2,1)}), bf16[2,32,1,128,4,128]{5,3,4,2,0,1:T(8,128)(2,1)}, u32[]{:S(2)}, u32[]{:S(2)}) async-start(bf16[2,32,1,128,4,128]{5,3,4,2,0,1:T(8,128)(2,1)} %copy.99), calls=%async_computation | async-start | bytes 16777216 | tf_op jit(solution)/shard_map/all_to_all | solution.py:52
  84.9 10.9 %reshape.509 = f32[9,128,18,128]{3,2,1,0:T(8,128)} reshape(bf16[1152,2304]{1,0:T(8,128)(2,1)} %param.5) | data formatting | bytes 15925248 | tf_op jit(solution)/shard_map/reshape | solution.py:58
  95.7 11.0 %copy.100 = f32[9,128,18,128]{3,1,2,0:T(8,128)} copy(f32[9,128,18,128]{3,2,1,0:T(8,128)} %reshape.509) | data formatting | bytes 21233664 | tf_op jit(solution)/shard_map/reshape | solution.py:58
  106.8 0.6 gather_fusion.1
  107.6 0.8 sort.69
  108.7 0.8 gather_fusion.5
  109.9 0.7 gather_fusion.4
  111.4 69.6 %all-to-all-done = bf16[2,32,1,128,4,128]{5,3,4,2,0,1:T(8,128)(2,1)} async-done(((bf16[2,32,1,128,4,128]{5,3,4,2,0,1:T(8,128)(2,1)}), bf16[2,32,1,128,4,128]{5,3,4,2,0,1:T(8,128)(2,1)}, u32[]{:S(2)}, u32[]{:S(2)}) %all-to-all-start) | async-done | bytes 8388640 | tf_op jit(solution)/shard_map/all_to_all | solution.py:52
  181.0 3.8 fusion.18
  184.8 4.3 convert.5
  189.1 4.3 convert.6
  193.4 27.2 %scatter_fusion = f32[9,128,18,128]{3,1,2,0:T(8,128)} fusion(f32[9,128,18,128]{3,1,2,0:T(8,128)} %copy.100, s32[128]{0:T(128)S(1)} %reshape.570, f32[128,128,128]{2,1,0:T(8,128)} %bitcast.155), kind=kCustom, calls=%fused_computation.8 | custom fusion | flops 2097152 | bytes 25166848 | tf_op jit(solution)/shard_map/scatter-add | solution.py:63
  220.6 27.4 %scatter_fusion.1 = f32[9,128,18,128]{3,1,2,0:T(8,128)} fusion(f32[9,128,18,128]{3,1,2,0:T(8,128)} %scatter_fusion, s32[128]{0:T(128)S(1)} %reshape.576, f32[128,128,128]{2,1,0:T(8,128)} %bitcast.156), kind=kCustom, calls=%fused_computation.9 | custom fusion | flops 2097152 | bytes 25166848 | tf_op jit(solution)/shard_map/scatter-add | solution.py:63
  248.0 15.3 %copy.102 = f32[9,128,18,128]{3,2,1,0:T(8,128)} copy(f32[9,128,18,128]{3,1,2,0:T(8,128)} %scatter_fusion.1) | data formatting | bytes 21233664 | tf_op jit(solution)/shard_map/scatter-add | solution.py:63
  263.4 11.7 %copy.119 = f32[144,8,18,128]{3,1,2,0:T(8,128)} copy(f32[144,8,18,128]{3,2,1,0:T(8,128)} %bitcast.154) | data formatting | bytes 21233664
  275.1 490.8 %while.17 = (s32[]{:T(128)}, f32[1152,2304]{1,0:T(8,128)}, s32[]{:T(128)}, s32[]{:T(128)}, s32[]{:T(128)}, /*index=5*/s32[]{:T(128)}, s32[]{:T(128)}, s32[]{:T(1...) while((s32[]{:T(128)}, f32[1152,2304]{1,0:T(8,128)}, ...), condition=%wide.region_13.14_spmd.clone, body=%wide.region_6.13_spmd.clone.sunk | while | flops 4307976192 | bytes 43714316 | solution.py:105
  275.3 1.9 dynamic-slice_select_fusion.4
  277.4 45.2 %all-reduce.7.cloned.1.call-done = f32[1152,128]{1,0:T(8,128)} async-done(((f32[1152,128]{1,0:T(8,128)}), f32[1152,128]{1,0:T(8,128)}) %all-reduce.7.cloned.1.call-update) | async-done | bytes 589840 | tf_op jit(solution)/shard_map/while/body/eval_jaxpr/psum | solution.py:12
  322.6 1.5 dynamic-slice_select_fusion.5
  324.1 73.2 %all-reduce.9.cloned.1.call-done = f32[128,128]{1,0:T(8,128)} async-done(((f32[128,128]{1,0:T(8,128)}), f32[128,128]{1,0:T(8,128)}) %all-reduce.9.cloned.1.call-update) | async-done | bytes 65552 | tf_op jit(solution)/shard_map/while/body/eval_jaxpr/psum | solution.py:12
  397.3 0.9 copy.121
  398.3 0.9 fusion.31
  399.1 11.7 %cholesky.64 = f32[128,128]{1,0:T(8,128)S(1)} custom-call(f32[128,128]{1,0:T(8,128)S(1)} %fusion.31), custom_call_target="Cholesky" | custom-call | tf_op jit(solution)/shard_map/while/body/eval_jaxpr/jit(cholesky)/cholesky | solution.py:75
  410.9 0.6 compare_reduce_fusion.2
  411.5 0.6 select_bitcast_fusion.2
  412.1 9.8 %custom-call.44 = f32[1,128,128]{1,2,0:T(8,128)S(1)} custom-call(f32[1,128,128]{2,1,0:T(8,128)S(1)} %get-tuple-element.255), custom_call_target="InvertDiagBlocksLowerTriangular" | custom-call | tf_op jit(solution)/shard_map/while/body/eval_jaxpr/triangular_solve | solution.py:76
  421.9 1.7 broadcast_select_fusion.7
  423.6 1.1 broadcast_select_fusion.8
  424.7 80.9 %all-reduce.11.cloned.1.call-done = (f32[9,1,128,128]{3,2,1,0:T(8,128)}, f32[9,1,128,128]{3,2,1,0:T(8,128)}) async-done(((f32[9,1,128,128]{3,2,1,0:T(8,128)}, f32[9,1,128,128]{3,2,1,0:T(8,128)}), (f32[9,1,128,128]{3,2,1,0:T(8,128)}, f32[9,1,128,128]{3,2,1,0:T(8,128)})) %all-reduce.11.cloned.1.call-update) | async-done | bytes 1179664 | tf_op jit(solution)/shard_map/while/body/eval_jaxpr/psum | solution.py:12
  505.6 1.3 pad_maximum_fusion.2
  506.9 13.0 %convolution_subtract_fusion.2 = f32[1152,2304]{1,0:T(8,128)} fusion(f32[1152,2304]{1,0:T(8,128)} %get-tuple-element.284, f32[1152,128]{1,0:T(8,128)S(1)} %bitcast.150, f32[2304,128]{1,0:T(8,128)S(1)} %bitcast.151), kind=kOutput, calls=%fused_computation.11.clone.1 | convolution fusion | flops 4079517696 | bytes 23003136 | tf_op jit(solution)/shard_map/while/body/eval_jaxpr/dot_general | solution.py:94
  519.9 1.9 constant_dynamic-update-slice_fusion.2
  521.9 1.9 dynamic-slice_select_fusion.4
  523.9 42.7 %all-reduce.7.cloned.1.call-done = f32[1152,128]{1,0:T(8,128)} async-done(((f32[1152,128]{1,0:T(8,128)}), f32[1152,128]{1,0:T(8,128)}) %all-reduce.7.cloned.1.call-update) | async-done | bytes 589840 | tf_op jit(solution)/shard_map/while/body/eval_jaxpr/psum | solution.py:12
  566.6 1.5 dynamic-slice_select_fusion.5
  568.2 73.1 %all-reduce.9.cloned.1.call-done = f32[128,128]{1,0:T(8,128)} async-done(((f32[128,128]{1,0:T(8,128)}), f32[128,128]{1,0:T(8,128)}) %all-reduce.9.cloned.1.call-update) | async-done | bytes 65552 | tf_op jit(solution)/shard_map/while/body/eval_jaxpr/psum | solution.py:12
  641.3 0.9 copy.121
  642.2 0.9 fusion.31
  643.0 11.7 %cholesky.64 = f32[128,128]{1,0:T(8,128)S(1)} custom-call(f32[128,128]{1,0:T(8,128)S(1)} %fusion.31), custom_call_target="Cholesky" | custom-call | tf_op jit(solution)/shard_map/while/body/eval_jaxpr/jit(cholesky)/cholesky | solution.py:75
  654.8 0.6 compare_reduce_fusion.2
  655.4 0.6 select_bitcast_fusion.2
  656.0 9.8 %custom-call.44 = f32[1,128,128]{1,2,0:T(8,128)S(1)} custom-call(f32[1,128,128]{2,1,0:T(8,128)S(1)} %get-tuple-element.255), custom_call_target="InvertDiagBlocksLowerTriangular" | custom-call | tf_op jit(solution)/shard_map/while/body/eval_jaxpr/triangular_solve | solution.py:76
  665.8 1.7 broadcast_select_fusion.7
  667.5 1.1 broadcast_select_fusion.8
  668.7 80.8 %all-reduce.11.cloned.1.call-done = (f32[9,1,128,128]{3,2,1,0:T(8,128)}, f32[9,1,128,128]{3,2,1,0:T(8,128)}) async-done(((f32[9,1,128,128]{3,2,1,0:T(8,128)}, f32[9,1,128,128]{3,2,1,0:T(8,128)}), (f32[9,1,128,128]{3,2,1,0:T(8,128)}, f32[9,1,128,128]{3,2,1,0:T(8,128)})) %all-reduce.11.cloned.1.call-update) | async-done | bytes 1179664 | tf_op jit(solution)/shard_map/while/body/eval_jaxpr/psum | solution.py:12
  749.4 1.3 pad_maximum_fusion.2
  750.8 13.0 %convolution_subtract_fusion.2 = f32[1152,2304]{1,0:T(8,128)} fusion(f32[1152,2304]{1,0:T(8,128)} %get-tuple-element.284, f32[1152,128]{1,0:T(8,128)S(1)} %bitcast.150, f32[2304,128]{1,0:T(8,128)S(1)} %bitcast.151), kind=kOutput, calls=%fused_computation.11.clone.1 | convolution fusion | flops 4079517696 | bytes 23003136 | tf_op jit(solution)/shard_map/while/body/eval_jaxpr/dot_general | solution.py:94
  763.7 1.9 constant_dynamic-update-slice_fusion.2
  765.9 1.0 broadcast_in_dim.226
  766.9 9.9 %bitcast_select_fusion.1 = f32[1152,2304]{1,0:T(8,128)} fusion(f32[1152,2304]{1,0:T(8,128)} %get-tuple-element.166, pred[144,8,18,128]{3,2,1,0:T(8,128)(4,1)S(1)} %bitcast.165), kind=kLoop, calls=%fused_computation.36 | loop fusion | flops 2654208 | bytes 23887872 | tf_op jit(solution)/shard_map/jit(_where)/select_n | solution.py:108
  (87 shorter events, 3.1 us)
Async XLA Ops:
  76.5 104.5 %all-to-all-start = ((bf16[2,32,1,128,4,128]{5,3,4,2,0,1:T(8,128)(2,1)}), bf16[2,32,1,128,4,128]{5,3,4,2,0,1:T(8,128)(2,1)}, u32[]{:S(2)}, u32[]{:S(2)}) async-start(bf16[2,32,1,128,4,128]{5,3,4,2,0,1:T(8,128)(2,1)} %copy.99), calls=%async_computation | async-start | bytes 16777216 | tf_op jit(solution)/shard_map/all_to_all | solution.py:52
  275.3 47.3 %all-reduce.7.cloned.1.call-start = ((), (), s32[]{:S(2)}) async-start(), calls=%async_computation.1 | async-start | bytes 1179648 | tf_op jit(solution)/shard_map/while/body/eval_jaxpr/psum | solution.py:12
  277.3 120.1 %all-reduce.9.cloned.1.call-start = ((), (), s32[]{:S(2)}) async-start(), calls=%async_computation.2 | async-start | bytes 131072 | tf_op jit(solution)/shard_map/while/body/eval_jaxpr/psum | solution.py:12
  324.0 181.6 %all-reduce.11.cloned.1.call-start = ((), (), s32[]{:S(2)}) async-start(), calls=%async_computation.3 | async-start | bytes 2359296 | tf_op jit(solution)/shard_map/while/body/eval_jaxpr/psum | solution.py:12
  521.9 44.8 %all-reduce.7.cloned.1.call-start = ((), (), s32[]{:S(2)}) async-start(), calls=%async_computation.1 | async-start | bytes 1179648 | tf_op jit(solution)/shard_map/while/body/eval_jaxpr/psum | solution.py:12
  523.8 117.4 %all-reduce.9.cloned.1.call-start = ((), (), s32[]{:S(2)}) async-start(), calls=%async_computation.2 | async-start | bytes 131072 | tf_op jit(solution)/shard_map/while/body/eval_jaxpr/psum | solution.py:12
  568.1 181.3 %all-reduce.11.cloned.1.call-start = ((), (), s32[]{:S(2)}) async-start(), calls=%async_computation.3 | async-start | bytes 2359296 | tf_op jit(solution)/shard_map/while/body/eval_jaxpr/psum | solution.py:12
Sparse Core Ops, SparseCore 0:
  278.6 43.9 all-reduce.6
  325.0 72.2 all-reduce.8
  424.9 80.7 all-reduce.10
  524.9 41.6 all-reduce.6
  568.9 72.2 all-reduce.8
  668.8 80.5 all-reduce.10
where the time goes:
time: 794 us; the launch traced here: 784 us
  waiting for transfers between devices  466 us (59%)
  other arithmetic  156 us (20%)
  local copies, waits for them, and re-layouts  110 us (14%)
  matrix products  29.3 us (4%)
  between operations  13.9 us (2%)
  starting transfers between devices  8.58 us (1%)
    psum x6, waiting for transfers between devices, broadcast(): return lax.psum(kept, axis)  396 us
    all_to_all x1, waiting for transfers between devices, shards(): lax.all_to_all(outgoing, ('row', 'col'), split_axis=1, concat_axis=1, til...  69.6 us
    scatter-add x2, other arithmetic, shards(): assembled = assembled.at[row_dest[child_index][:, None], :, col_dest[chil...  54.6 us
    dot_general x2, matrix products, eliminate(): lax.dot_general(below_rows, across_cols, (((1,), (1,)), ((), ())), precis...  26 us
    another operation x6, other arithmetic, eliminate(): diag_factor = jnp.tril(jnp.linalg.cholesky(diag_block))  24.8 us
    unnamed x5, local copies, waits for them, and re-layouts  22.4 us
    reshape x2, local copies, waits for them, and re-layouts, shards(): front_entries.astype(jnp.float32).reshape(front_rows, BLK, front_cols, BLK)  21.8 us
    another operation x4, other arithmetic, eliminate(): lax.linalg.triangular_solve(diag_factor, column, left_side=False, lower=T...  20.8 us
  transfers between devices with their start and end apart: 7, of which 7 were waited for; matrix products, arithmetic and copies ran while one was open for 3% of the time, Pallas kernels for 0%

commit v1 on v0

--- a/solution.py
+++ b/solution.py
@@ -9,7 +9,7 @@
 
 def broadcast(value, axis, source):
     kept = jnp.where(lax.axis_index(axis) == source, value, 0).astype(value.dtype)
-    return lax.psum(kept, axis)
+    return jnp.sum(lax.all_gather(kept, axis), axis=0)
 
 
 def arrivals(child_maps, axis_size, own_index, blocks):

time: 794 us -> 921 us (1.16)
  waiting for transfers between devices: 466 us -> 527 us
  blocking collectives: 0 us -> 60.3 us
    all_gather x0 -> x6, waiting for transfers between devices: none -> 456 us  [broadcast(): return jnp.sum(lax.all_gather(kept, axis), axis=0)]
    psum x6 -> x0, waiting for transfers between devices: 396 us -> none  [broadcast(): return lax.psum(kept, axis)]
    all_gather x0 -> x2, blocking collectives: none -> 60.3 us  [broadcast(): return jnp.sum(lax.all_gather(kept, axis), axis=0)]
    reduce_sum x0 -> x8, other arithmetic: none -> 14.3 us  [broadcast(): return jnp.sum(lax.all_gather(kept, axis), axis=0)]
where the time goes in v1:
time: 921 us; the launch traced here: 910 us
  waiting for transfers between devices  527 us (57%)
  other arithmetic  163 us (18%)
  local copies, waits for them, and re-layouts  108 us (12%)
  blocking collectives  60.3 us (7%)
  matrix products  28.8 us (3%)
  between operations  13.9 us (2%)
    all_gather x6, waiting for transfers between devices, broadcast(): return jnp.sum(lax.all_gather(kept, axis), axis=0)  456 us
    all_to_all x1, waiting for transfers between devices, shards(): lax.all_to_all(outgoing, ('row', 'col'), split_axis=1, concat_axis=1, til...  69.6 us
    all_gather x2, blocking collectives, broadcast(): return jnp.sum(lax.all_gather(kept, axis), axis=0)  60.3 us
    scatter-add x2, other arithmetic, shards(): assembled = assembled.at[row_dest[child_index][:, None], :, col_dest[chil...  54.6 us
    dot_general x2, matrix products, eliminate(): lax.dot_general(below_rows, across_cols, (((1,), (1,)), ((), ())), precis...  26 us
    another operation x6, other arithmetic, eliminate(): diag_factor = jnp.tril(jnp.linalg.cholesky(diag_block))  24.9 us
    unnamed x5, local copies, waits for them, and re-layouts  22.4 us
    reshape x2, local copies, waits for them, and re-layouts, shards(): front_entries.astype(jnp.float32).reshape(front_rows, BLK, front_cols, BLK)  21.8 us
  transfers between devices with their start and end apart: 7, of which 7 were waited for; matrix products, arithmetic and copies ran while one was open for 3% of the time, Pallas kernels for 0%

profile of v1, /device:TPU:0, one launch (start us, length us, event | category | flops | bytes accessed | tf_op | source)
XLA Modules:
  0.0 910.2 jit_solution(13669976361922222407)
XLA Ops:
  6.5 0.8 copy.71
  7.9 0.7 sort.71
  8.6 0.6 gather_fusion.2
  9.2 0.7 sort.70
  10.0 0.6 gather_fusion
  10.9 0.7 sort.68
  11.7 9.9 %copy.108 = bf16[256,8,16,128]{3,2,1,0:T(8,128)(2,1)} copy(bf16[256,8,16,128]{3,1,2,0:T(8,128)(2,1)} %bitcast.174) | data formatting | bytes 16777216
  22.0 8.3 gather_fusion.6
  30.3 8.8 copy_select_fusion
  39.1 8.6 gather_fusion.7
  47.7 10.5 %copy.92 = bf16[2,8,128,16,128]{4,2,3,1,0:T(8,128)(2,1)} copy(bf16[2,8,128,16,128]{4,2,1,3,0:T(8,128)(2,1)} %bitcast.166) | data formatting | bytes 16777216 | tf_op jit(solution)/shard_map/jit(take_along_axis)/gather | solution.py:47
  58.3 7.7 broadcast_select_fusion.4
  66.0 10.5 %copy.93 = bf16[2,32,1,128,4,128]{5,3,4,2,0,1:T(8,128)(2,1)} copy(bf16[2,32,1,128,4,128]{5,3,4,2,1,0:T(8,128)(2,1)} %bitcast.170) | data formatting | bytes 16777216 | tf_op jit(solution)/shard_map/reshape | solution.py:49
  76.5 8.4 all-to-all-start
  84.9 10.9 %reshape.547 = f32[9,128,18,128]{3,2,1,0:T(8,128)} reshape(bf16[1152,2304]{1,0:T(8,128)(2,1)} %param.5) | data formatting | bytes 15925248 | tf_op jit(solution)/shard_map/reshape | solution.py:58
  95.7 11.0 %copy.94 = f32[9,128,18,128]{3,1,2,0:T(8,128)} copy(f32[9,128,18,128]{3,2,1,0:T(8,128)} %reshape.547) | data formatting | bytes 21233664 | tf_op jit(solution)/shard_map/reshape | solution.py:58
  106.8 0.6 gather_fusion.1
  107.6 0.8 sort.69
  108.7 0.8 gather_fusion.5
  109.9 0.7 gather_fusion.4
  111.4 69.6 %all-to-all-done = bf16[2,32,1,128,4,128]{5,3,4,2,0,1:T(8,128)(2,1)} async-done(((bf16[2,32,1,128,4,128]{5,3,4,2,0,1:T(8,128)(2,1)}), bf16[2,32,1,128,4,128]{5,3,4,2,0,1:T(8,128)(2,1)}, u32[]{:S(2)}, u32[]{:S(2)}) %all-to-all-start) | async-done | bytes 8388640 | tf_op jit(solution)/shard_map/all_to_all | solution.py:52
  181.0 3.8 fusion.18
  184.8 4.3 convert.5
  189.1 4.3 convert.6
  193.4 27.2 %scatter_fusion = f32[9,128,18,128]{3,1,2,0:T(8,128)} fusion(f32[9,128,18,128]{3,1,2,0:T(8,128)} %copy.94, s32[128]{0:T(128)S(1)} %reshape.608, f32[128,128,128]{2,1,0:T(8,128)} %bitcast.164), kind=kCustom, calls=%fused_computation.8 | custom fusion | flops 2097152 | bytes 25166848 | tf_op jit(solution)/shard_map/scatter-add | solution.py:63
  220.6 27.4 %scatter_fusion.1 = f32[9,128,18,128]{3,1,2,0:T(8,128)} fusion(f32[9,128,18,128]{3,1,2,0:T(8,128)} %scatter_fusion, s32[128]{0:T(128)S(1)} %reshape.614, f32[128,128,128]{2,1,0:T(8,128)} %bitcast.165), kind=kCustom, calls=%fused_computation.9 | custom fusion | flops 2097152 | bytes 25166848 | tf_op jit(solution)/shard_map/scatter-add | solution.py:63
  248.0 15.3 %copy.96 = f32[9,128,18,128]{3,2,1,0:T(8,128)} copy(f32[9,128,18,128]{3,1,2,0:T(8,128)} %scatter_fusion.1) | data formatting | bytes 21233664 | tf_op jit(solution)/shard_map/scatter-add | solution.py:63
  263.4 11.7 %copy.113 = f32[144,8,18,128]{3,1,2,0:T(8,128)} copy(f32[144,8,18,128]{3,2,1,0:T(8,128)} %bitcast.162) | data formatting | bytes 21233664
  275.1 617.1 %while.17 = (s32[]{:T(128)}, f32[1152,2304]{1,0:T(8,128)}, s32[]{:T(128)}, s32[]{:T(128)}, s32[]{:T(128)}, /*index=5*/s32[]{:T(128)}, u32[]{:T(128)}, u32[]{:T(1...) while((s32[]{:T(128)}, f32[1152,2304]{1,0:T(8,128)}, ...), condition=%wide.region_13.14_spmd.clone, body=%wide.region_6.13_spmd.clone.sunk | while | flops 4310138880 | bytes 88147752 | solution.py:105
  275.3 1.9 dynamic-slice_select_fusion.4
  277.4 30.0 %all-gather.12.cloned.1.call-done = f32[4608,128]{1,0:T(8,128)} async-done(((f32[1152,128]{1,0:T(8,128)}), f32[4608,128]{1,0:T(8,128)}) %all-gather.12.cloned.1.call-update) | async-done | bytes 2359312 | tf_op jit(solution)/shard_map/while/body/eval_jaxpr/all_gather | solution.py:12
  307.4 1.9 reduce_sum.76
  309.3 30.2 %all-gather.7 = f32[1024,128]{1,0:T(8,128)S(1)} all-gather(f32[128,128]{1,0:T(8,128)S(1)} %dynamic-slice_select_fusion.5), channel_id=3, replica_groups=mesh['front'=4,'row'=8,'col'=4] {'row'}, dimensions={0}, use_global_device_ids=true | all-gather | bytes 589824 | tf_op jit(solution)/shard_map/while/body/eval_jaxpr/all_gather | solution.py:12
  339.6 11.7 %cholesky.64 = f32[128,128]{1,0:T(8,128)S(1)} custom-call(f32[128,128]{1,0:T(8,128)S(1)} %fusion.31), custom_call_target="Cholesky" | custom-call | tf_op jit(solution)/shard_map/while/body/eval_jaxpr/jit(cholesky)/cholesky | solution.py:75
  351.3 0.7 compare_reduce_fusion.2
  352.0 0.7 select_bitcast_fusion.2
  352.8 9.8 %custom-call.44 = f32[1,128,128]{1,2,0:T(8,128)S(1)} custom-call(f32[1,128,128]{2,1,0:T(8,128)S(1)} %get-tuple-element.249), custom_call_target="InvertDiagBlocksLowerTriangular" | custom-call | tf_op jit(solution)/shard_map/while/body/eval_jaxpr/triangular_solve | solution.py:76
  362.6 1.4 broadcast_select_fusion.8
  364.0 0.8 broadcast_select_fusion.9
  364.9 0.7 all-gather.16.cloned.1.call-update
  365.6 99.1 %all-gather.14.cloned.1.call-done = f32[8,1152,128]{2,1,0:T(8,128)} async-done(((f32[1,1152,128]{2,1,0:T(8,128)}), f32[8,1152,128]{2,1,0:T(8,128)}) %all-gather.14.cloned.1.call-update) | async-done | bytes 4718608 | tf_op jit(solution)/shard_map/while/body/eval_jaxpr/all_gather | solution.py:12
  464.7 2.6 reduce_sum.78
  467.3 99.6 %all-gather.16.cloned.1.call-done = f32[8,1152,128]{2,1,0:T(8,128)} async-done(((f32[1,1152,128]{2,1,0:T(8,128)}), f32[8,1152,128]{2,1,0:T(8,128)}) %all-gather.16.cloned.1.call-update) | async-done | bytes 4718608 | tf_op jit(solution)/shard_map/while/body/eval_jaxpr/all_gather | solution.py:12
  567.0 2.6 reduce_sum.79
  569.7 13.0 %convolution_subtract_fusion.2 = f32[1152,2304]{1,0:T(8,128)} fusion(f32[1152,2304]{1,0:T(8,128)} %get-tuple-element.276, f32[1152,128]{1,0:T(8,128)S(1)} %bitcast.154, f32[2304,128]{1,0:T(8,128)S(1)} %bitcast.155), kind=kOutput, calls=%fused_computation.11.clone.1 | convolution fusion | flops 4079517696 | bytes 23003136 | tf_op jit(solution)/shard_map/while/body/eval_jaxpr/dot_general | solution.py:94
  582.7 1.9 constant_dynamic-update-slice_fusion.2
  584.6 1.9 dynamic-slice_select_fusion.4
  586.7 28.2 %all-gather.12.cloned.1.call-done = f32[4608,128]{1,0:T(8,128)} async-done(((f32[1152,128]{1,0:T(8,128)}), f32[4608,128]{1,0:T(8,128)}) %all-gather.12.cloned.1.call-update) | async-done | bytes 2359312 | tf_op jit(solution)/shard_map/while/body/eval_jaxpr/all_gather | solution.py:12
  614.9 1.9 reduce_sum.76
  616.8 30.2 %all-gather.7 = f32[1024,128]{1,0:T(8,128)S(1)} all-gather(f32[128,128]{1,0:T(8,128)S(1)} %dynamic-slice_select_fusion.5), channel_id=3, replica_groups=mesh['front'=4,'row'=8,'col'=4] {'row'}, dimensions={0}, use_global_device_ids=true | all-gather | bytes 589824 | tf_op jit(solution)/shard_map/while/body/eval_jaxpr/all_gather | solution.py:12
  647.1 11.7 %cholesky.64 = f32[128,128]{1,0:T(8,128)S(1)} custom-call(f32[128,128]{1,0:T(8,128)S(1)} %fusion.31), custom_call_target="Cholesky" | custom-call | tf_op jit(solution)/shard_map/while/body/eval_jaxpr/jit(cholesky)/cholesky | solution.py:75
  658.8 0.7 compare_reduce_fusion.2
  659.5 0.7 select_bitcast_fusion.2
  660.3 9.8 %custom-call.44 = f32[1,128,128]{1,2,0:T(8,128)S(1)} custom-call(f32[1,128,128]{2,1,0:T(8,128)S(1)} %get-tuple-element.249), custom_call_target="InvertDiagBlocksLowerTriangular" | custom-call | tf_op jit(solution)/shard_map/while/body/eval_jaxpr/triangular_solve | solution.py:76
  670.1 1.4 broadcast_select_fusion.8
  671.5 0.8 broadcast_select_fusion.9
  673.0 99.2 %all-gather.14.cloned.1.call-done = f32[8,1152,128]{2,1,0:T(8,128)} async-done(((f32[1,1152,128]{2,1,0:T(8,128)}), f32[8,1152,128]{2,1,0:T(8,128)}) %all-gather.14.cloned.1.call-update) | async-done | bytes 4718608 | tf_op jit(solution)/shard_map/while/body/eval_jaxpr/all_gather | solution.py:12
  772.2 2.6 reduce_sum.78
  774.8 99.5 %all-gather.16.cloned.1.call-done = f32[8,1152,128]{2,1,0:T(8,128)} async-done(((f32[1,1152,128]{2,1,0:T(8,128)}), f32[8,1152,128]{2,1,0:T(8,128)}) %all-gather.16.cloned.1.call-update) | async-done | bytes 4718608 | tf_op jit(solution)/shard_map/while/body/eval_jaxpr/all_gather | solution.py:12
  874.3 2.6 reduce_sum.79
  877.0 13.0 %convolution_subtract_fusion.2 = f32[1152,2304]{1,0:T(8,128)} fusion(f32[1152,2304]{1,0:T(8,128)} %get-tuple-element.276, f32[1152,128]{1,0:T(8,128)S(1)} %bitcast.154, f32[2304,128]{1,0:T(8,128)S(1)} %bitcast.155), kind=kOutput, calls=%fused_computation.11.clone.1 | convolution fusion | flops 4079517696 | bytes 23003136 | tf_op jit(solution)/shard_map/while/body/eval_jaxpr/dot_general | solution.py:94
  890.0 1.9 constant_dynamic-update-slice_fusion.2
  892.2 1.0 broadcast_in_dim.226
  893.2 9.9 %bitcast_select_fusion.1 = f32[1152,2304]{1,0:T(8,128)} fusion(f32[1152,2304]{1,0:T(8,128)} %get-tuple-element.166, pred[144,8,18,128]{3,2,1,0:T(8,128)(4,1)S(1)} %bitcast.173), kind=kLoop, calls=%fused_computation.36 | loop fusion | flops 2654208 | bytes 23887872 | tf_op jit(solution)/shard_map/jit(_where)/select_n | solution.py:108
  (97 shorter events, 4.6 us)
Async XLA Ops:
  76.5 104.5 %all-to-all-start = ((bf16[2,32,1,128,4,128]{5,3,4,2,0,1:T(8,128)(2,1)}), bf16[2,32,1,128,4,128]{5,3,4,2,0,1:T(8,128)(2,1)}, u32[]{:S(2)}, u32[]{:S(2)}) async-start(bf16[2,32,1,128,4,128]{5,3,4,2,0,1:T(8,128)(2,1)} %copy.93), calls=%async_computation | async-start | bytes 16777216 | tf_op jit(solution)/shard_map/all_to_all | solution.py:52
  275.3 32.1 %all-gather.12.cloned.1.call-start = ((), (), s32[]{:S(2)}) async-start(), calls=%async_computation.1 | async-start | bytes 2949120 | tf_op jit(solution)/shard_map/while/body/eval_jaxpr/all_gather | solution.py:12
  277.3 187.4 %all-gather.14.cloned.1.call-start = ((), (), s32[]{:S(2)}) async-start(), calls=%async_computation.2 | async-start | bytes 5308416 | tf_op jit(solution)/shard_map/while/body/eval_jaxpr/all_gather | solution.py:12
  364.9 202.1 %all-gather.16.cloned.1.call-start = ((), (), s32[]{:S(2)}) async-start(), calls=%async_computation.3 | async-start | bytes 5308416 | tf_op jit(solution)/shard_map/while/body/eval_jaxpr/all_gather | solution.py:12
  584.6 30.3 %all-gather.12.cloned.1.call-start = ((), (), s32[]{:S(2)}) async-start(), calls=%async_computation.1 | async-start | bytes 2949120 | tf_op jit(solution)/shard_map/while/body/eval_jaxpr/all_gather | solution.py:12
  586.5 185.6 %all-gather.14.cloned.1.call-start = ((), (), s32[]{:S(2)}) async-start(), calls=%async_computation.2 | async-start | bytes 5308416 | tf_op jit(solution)/shard_map/while/body/eval_jaxpr/all_gather | solution.py:12
  672.4 201.9 %all-gather.16.cloned.1.call-start = ((), (), s32[]{:S(2)}) async-start(), calls=%async_computation.3 | async-start | bytes 5308416 | tf_op jit(solution)/shard_map/while/body/eval_jaxpr/all_gather | solution.py:12
Sparse Core Ops, SparseCore 0:
  277.8 29.5 all-gather.11
  365.0 99.6 all-gather.13
  466.3 100.5 all-gather.15
  586.8 28.0 all-gather.11
  672.5 99.6 all-gather.13
  773.7 100.5 all-gather.15
